TPU v7x, 32 devices: a whole 2x2x4 slice. The times are simulated.
32 devices in a mesh: epoch: 4 (over z), vel: 8 (over y, x, core).
Axes of the slice: x: 2, y: 2, z: 4, core: 2. Of those that a mesh axis runs over, the one named last changes fastest.
Arguments:
- science: float32 [8, 32, 1024], P('epoch', 'vel'), may hold values from -6 to 6
- variance: float32 [8, 32, 1024], P('epoch', 'vel'), may hold values from 0.25 to 4
- psf: float32 [8, 9], P('epoch'), may hold values from 0.05 to 1
- shifts: int32 [2, 8, 8], P(None, None, 'vel'), may hold values from -16 to 16, as said below
Outputs:
- likelihood: float32 [8, 32, 1024], P('vel', 'epoch')
Inputs may be any that keep to these rules, and one draw needn't show every extreme that they name: For each velocity, the shifts of epoch e are the floor of the velocity's integer rates times the epoch's time over the span of the times; the first epoch's shifts are zero, and times rise with the epoch.
All inputs are finite; a program needn't handle non-finite values.
Results may differ from a plain program's by a relative error of at most 0.0003.
Values sent between devices are 32-bit elements; how exact they have to be, the bound alone decides.
No kernel may reach another device: no remote copies, remote signals or barrier semaphores. Data moves between devices by JAX's collectives and lax.ppermute only.
A program may use at most 64 MiB of HBM per device.

v0:
```python
import jax
import jax.numpy as jnp
from jax import lax
from jax.sharding import PartitionSpec as P

MAXS = 16


def extended(block, sides, width):
    for axis, dim in sides:
        count = lax.axis_size(axis)
        forward = [(i, i + 1) for i in range(count - 1)]
        backward = [(target, source) for source, target in forward]
        low = lax.ppermute(
            lax.slice_in_dim(block, block.shape[dim] - width, None, axis=dim), axis, forward
        )
        high = lax.ppermute(lax.slice_in_dim(block, 0, width, axis=dim), axis, backward)
        block = jnp.concatenate([low, block, high], axis=dim)
    return block


def filter_columns(pairing, weights):
    radius = weights.shape[2] // 2
    breadth = pairing.shape[3]
    padded = jnp.pad(pairing, ((0, 0), (0, 0), (0, 0), (radius, radius)))
    summed = jnp.zeros_like(pairing)
    for offset in range(weights.shape[2]):
        summed = (
            summed + weights[:, :, offset, None, None] * padded[:, :, :, offset : offset + breadth]
        )
    return summed


def filter_rows(rimmed, weights, height):
    summed = jnp.zeros(rimmed.shape[:2] + (height, rimmed.shape[3]), jnp.float32)
    for offset in range(weights.shape[2]):
        summed = (
            summed + weights[:, :, offset, None, None] * rimmed[:, :, offset : offset + height, :]
        )
    return summed


def per_device(science, variance, psf, shifts):
    slots = science.shape[0]
    height = science.shape[1]
    breadth = science.shape[2]
    radius = psf.shape[1] // 2
    pairing = jnp.stack([science / variance, 1.0 / variance], axis=1)
    weights = jnp.stack([psf, psf * psf], axis=1)
    columns_pass = filter_columns(pairing, weights)
    rimmed = extended(columns_pass, (("vel", 2),), radius)
    filtered = filter_rows(rimmed, weights, height)
    local_shifts = lax.dynamic_slice_in_dim(shifts, lax.axis_index("epoch") * slots, slots, 1)
    velocities = shifts.shape[2]
    gathered = lax.all_gather(filtered, "vel", axis=2, tiled=True)
    rows_all = gathered.shape[2]
    padded = jnp.pad(gathered, ((0, 0), (0, 0), (MAXS, MAXS), (MAXS, MAXS)))
    stacks = jnp.zeros((velocities, 2, rows_all, breadth), jnp.float32)
    for epoch_slot in range(slots):
        image = padded[epoch_slot]

        def window_at(shift_col, shift_row):
            return lax.dynamic_slice(
                image, (jnp.int32(0), MAXS + shift_row, MAXS + shift_col), (2, rows_all, breadth)
            )

        stacks = stacks + jax.vmap(window_at)(
            local_shifts[0, epoch_slot], local_shifts[1, epoch_slot]
        )
    mine = lax.psum_scatter(stacks, "epoch", scatter_dimension=2, tiled=True)
    return mine[:, 0] / jnp.sqrt(mine[:, 1])


def solution(mesh):
    return jax.shard_map(
        per_device,
        mesh=mesh,
        in_specs=(
            P("epoch", "vel", None),
            P("epoch", "vel", None),
            P("epoch", None),
            P(None, None, "vel"),
        ),
        out_specs=P("vel", "epoch", None),
        check_vma=False,
    )
```

profile of v0, /device:TPU:0, one launch (start us, length us, event | category | flops | bytes accessed | tf_op | source)
XLA Modules:
  0.0 81.5 jit_solution(1506419152563569825)
XLA Ops:
  6.5 0.0 all-reduce.5.cloned.1.call-start
  6.5 0.7 multiply_bitcast_fusion
  7.2 1.1 %fusion.26 = (f32[2,2,1]{2,0,1:T(2,128)S(1)}, f32[2,2,1]{2,0,1:T(2,128)S(1)}, f32[2,2,1]{2,0,1:T(2,128)S(1)}, f32[2,2,1]{2,0,1:T(2,128)S(1)}, f32[2,2,1]{2,0,1:T...) fusion(f32[2,1,9]{2,0,1:T(2,128)} %bitcast.58, ...), kind=kLoop, calls=%fused_computation.63 | loop fusion | flops 36 | bytes 288 | tf_op jit(solution)/shard_map/stack | solution.py:49
  8.3 0.1 copy.63
  8.4 0.1 copy.64
  8.5 0.1 copy.65
  8.6 0.1 copy.66
  8.7 0.1 copy.67
  8.8 0.1 copy.68
  8.9 0.1 copy.60
  9.0 0.1 copy.61
  9.1 0.1 copy.62
  9.2 0.8 divide_bitcast_fusion.1
  10.0 0.4 multiply_add_fusion
  10.4 2.4 %collective-permute-start = (f32[2,2,4,1024]{3,2,0,1:T(4,128)S(1)}, f32[2,2,4,1024]{3,2,0,1:T(4,128)S(1)}, u32[]{:S(2)}, u32[]{:S(2)}) collective-permute-start(f32[2,2,4,1024]{3,2,0,1:T(4,128)S(1)} %multiply_add_fusion), channel_id=1, source_target_pairs={{0,1},{1,2},{2,3},{3,4},{4,5},{5,6},{6,7},{8,9},{9,10},{10,11},{11... | collective-permute-start | bytes 196616 | tf_op jit(solution)/shard_map/ppermute | solution.py:14
  12.8 1.3 %collective-permute-start.1 = (f32[2,2,4,1024]{3,2,0,1:T(4,128)S(1)}, f32[2,2,4,1024]{3,2,0,1:T(4,128)S(1)}, u32[]{:S(2)}, u32[]{:S(2)}) collective-permute-start(f32[2,2,4,1024]{3,2,0,1:T(4,128)S(1)} %multiply_add_fusion), channel_id=1, source_target_pairs={{1,0},{2,1},{3,2},{4,3},{5,4},{6,5},{7,6},{9,8},{10,9},{11,10},{12... | collective-permute-start | bytes 196616 | tf_op jit(solution)/shard_map/ppermute | solution.py:17
  14.1 1.4 %constant_dynamic-slice_fusion = (s32[1,1,1]{1,2,0:T(1,128)}, s32[1,1,1]{1,2,0:T(1,128)}, s32[1,1,1]{1,2,0:T(1,128)}, s32[1,1,1]{1,2,0:T(1,128)}) fusion(s32[2,8,1]{1,2,0:T(1,128)} %param.7, s32[]{:T(128)S(6)} %select_n.15, s32[]{:T(128)S(6)} %add.166, s32[]{:T(128)S(6)} %add.168), kind=kLoop, calls=%fused_computation.71 | loop fusion | bytes 44 | tf_op jit(solution)/shard_map/slice | solution.py:68
  20.4 0.0 collective-permute-done
  20.5 0.0 collective-permute-done.1
  20.5 0.3 fusion.4
  20.7 0.1 copy.58
  20.8 14.1 %all_gather.3 = f32[2,2,32,1024]{3,1,0,2:T(2,128)S(1)} all-gather(f32[2,2,4,1024]{3,1,0,2:T(2,128)S(1)} %copy.58), channel_id=1, replica_groups=mesh['epoch'=4,'vel'=8] {'vel'}, dimensions={2}, use_global_device_ids=true | all-gather | bytes 589824 | tf_op jit(solution)/shard_map/all_gather | solution.py:55
  34.9 0.7 pad_slice_fusion.1
  35.6 0.0 copy-start
  35.7 1.3 %dynamic-slice_add_fusion = f32[1,2,32,1024]{3,1,0,2:T(2,128)} fusion(f32[1,2,64,1056]{3,1,0,2:T(2,128)S(1)} %get-tuple-element.28, s32[]{:T(128)} %bitcast.30, s32[]{:T(128)} %bitcast.33, f32[1,2,64,1056]{3,1,0,2:T(2,128)S(1)} %get-tuple-element.27, s32[]{:T(128)} %bitcast.24, s32[]{:T(128)} %bitcast.27), kind=kLoop, calls=%fused_computation.2 | loop fusion | flops 65536 | bytes 786448 | tf_op jit(solution)/shard_map/add | solution.py:67
  37.0 0.0 all-reduce.5.cloned.1.call-update
  37.0 0.0 copy-done
  37.0 0.6 dynamic-slice.10
  38.3 34.8 %all-reduce.5.cloned.1.call-done = f32[1,2,32,1024]{3,1,0,2:T(2,128)} async-done(((f32[1,2,32,1024]{3,1,0,2:T(2,128)}), f32[1,2,32,1024]{3,1,0,2:T(2,128)}) %all-reduce.5.cloned.1.call-update) | async-done | bytes 262160
  73.0 1.0 %fusion.24 = f32[1,8,1024]{2,0,1:T(1,128)S(1)} fusion(f32[1,2,32,1024]{3,1,0,2:T(2,128)} %all-reduce.5.cloned.1.call-done, u32[]{:T(128)S(6)} %convert, u32[]{:T(128)S(6)} %multiply.11), kind=kLoop, calls=%fused_computation.45 | loop fusion | flops 8192 | bytes 98312 | tf_op jit(solution)/shard_map/div | solution.py:71
  74.0 0.6 copy.59
  (1 shorter events, 0.0 us)
Async XLA Ops:
  6.5 66.5 %all-reduce.5.cloned.1.call-start = ((), (), s32[]{:S(2)}) async-start(), calls=%async_computation | async-start | bytes 524288
  10.4 10.0 %collective-permute-start = (f32[2,2,4,1024]{3,2,0,1:T(4,128)S(1)}, f32[2,2,4,1024]{3,2,0,1:T(4,128)S(1)}, u32[]{:S(2)}, u32[]{:S(2)}) collective-permute-start(f32[2,2,4,1024]{3,2,0,1:T(4,128)S(1)} %multiply_add_fusion), channel_id=1, source_target_pairs={{0,1},{1,2},{2,3},{3,4},{4,5},{5,6},{6,7},{8,9},{9,10},{10,11},{11... | collective-permute-start | bytes 196616 | tf_op jit(solution)/shard_map/ppermute | solution.py:14
  12.8 7.6 %collective-permute-start.1 = (f32[2,2,4,1024]{3,2,0,1:T(4,128)S(1)}, f32[2,2,4,1024]{3,2,0,1:T(4,128)S(1)}, u32[]{:S(2)}, u32[]{:S(2)}) collective-permute-start(f32[2,2,4,1024]{3,2,0,1:T(4,128)S(1)} %multiply_add_fusion), channel_id=1, source_target_pairs={{1,0},{2,1},{3,2},{4,3},{5,4},{6,5},{7,6},{9,8},{10,9},{11,10},{12... | collective-permute-start | bytes 196616 | tf_op jit(solution)/shard_map/ppermute | solution.py:17
  35.6 1.4 %copy-start = (u32[32]{0:T(128)S(1)}, u32[32]{0:T(128)}, u32[]{:S(2)}) copy-start(u32[32]{0:T(128)} %constant.89) | copy-start | bytes 388
Sparse Core Ops, SparseCore 0:
  37.1 35.8 all-reduce.4
where the time goes:
time: 81.9 us; the launch traced here: 81.5 us
  waiting for transfers between devices  34.8 us (42%)
  between operations  19.1 us (23%)
  blocking collectives  14.1 us (17%)
  other arithmetic  5.5 us (7%)
  local copies, waits for them, and re-layouts  4.27 us (5%)
  starting transfers between devices  3.69 us (5%)
    unnamed x2, waiting for transfers between devices  34.8 us
    all_gather x1, blocking collectives, per_device(): gathered = lax.all_gather(filtered, 'vel', axis=2, tiled=True)  14.1 us
    ppermute x1, starting transfers between devices, extended(): lax.ppermute(lax.slice_in_dim(block, block.shape[dim] - width, None, axis...  2.4 us
    another operation x2, other arithmetic, per_device(): weights = jnp.stack([psf, psf * psf], axis=1)  1.77 us
  transfers between devices with their start and end apart: 3, of which 1 were waited for; matrix products, arithmetic and copies ran while one was open for 2% of the time, Pallas kernels for 0%

commit v1 on v0

--- a/solution.py
+++ b/solution.py
@@ -52,7 +52,24 @@
     filtered = filter_rows(rimmed, weights, height)
     local_shifts = lax.dynamic_slice_in_dim(shifts, lax.axis_index("epoch") * slots, slots, 1)
     velocities = shifts.shape[2]
-    gathered = lax.all_gather(filtered, "vel", axis=2, tiled=True)
+    size, position, rows = (lax.axis_size("vel"), lax.axis_index("vel"), filtered.shape[2])
+    ahead = [(i_2, (i_2 + 1) % size) for i_2 in range(size)]
+    downward = [(i_2, (i_2 - 1) % size) for i_2 in range(size)]
+    out = jnp.zeros((*filtered.shape[:2], size * rows, *filtered.shape[2 + 1 :]), filtered.dtype)
+    out = lax.dynamic_update_slice_in_dim(out, filtered, position * rows, axis=2)
+    from_left = from_right = filtered
+    middle = size // 2
+    for lap in range(1, middle + 1):
+        from_left = lax.ppermute(from_left, "vel", ahead)
+        out = lax.dynamic_update_slice_in_dim(
+            out, from_left, (position - lap) % size * rows, axis=2
+        )
+        if lap < size - middle:
+            from_right = lax.ppermute(from_right, "vel", downward)
+            out = lax.dynamic_update_slice_in_dim(
+                out, from_right, (position + lap) % size * rows, axis=2
+            )
+    gathered = out
     rows_all = gathered.shape[2]
     padded = jnp.pad(gathered, ((0, 0), (0, 0), (MAXS, MAXS), (MAXS, MAXS)))
     stacks = jnp.zeros((velocities, 2, rows_all, breadth), jnp.float32)

time: 81.9 us -> 73.7 us (0.90)
  blocking collectives: 14.1 us -> 0 us
  starting transfers between devices: 3.69 us -> 12 us
  local copies, waits for them, and re-layouts: 4.27 us -> 1.97 us
    unnamed x2 -> x1, waiting for transfers between devices: 34.8 us -> 0.02 us
    reduce_scatter x0 -> x1, waiting for transfers between devices: none -> 22.9 us  [per_device(): mine = lax.psum_scatter(stacks, 'epoch', scatter_dimension=2, tiled=True)]
    all_gather x1 -> x0, blocking collectives: 14.1 us -> none  [per_device(): gathered = lax.all_gather(filtered, 'vel', axis=2, tiled=True)]
    ppermute x0 -> x7, starting transfers between devices: none -> 8.33 us  [the longest x3 4.78 us: per_device(): from_right = lax.ppermute(from_right, 'vel', downward)]
    ppermute x0 -> x7, waiting for transfers between devices: none -> 8.31 us  [the longest x4 8.3 us: per_device(): from_left = lax.ppermute(from_left, 'vel', ahead)]
    ppermute x1, waiting for transfers between devices: 0.01 us -> 3.93 us  [extended(): lax.ppermute(lax.slice_in_dim(block, 0, width, axis=dim), axis, backward)]
    slice x0 -> x9, local copies, waits for them, and re-layouts: none -> 0.88 us  [the longest x8 0.78 us: filter_columns(): weights[:, :, offset, None, None] * padded[:, :, :, offset:offset + breadth]]
    mul x9 -> x0, local copies, waits for them, and re-layouts: 0.88 us -> none  [the longest x8 0.78 us: filter_columns(): weights[:, :, offset, None, None] * padded[:, :, :, offset:offset + breadth]]
  transfers between devices with their start and end apart: 3 -> 10, of which waited for: 1 -> 5; matrix products, arithmetic and copies ran while one was open for 2% -> 1% of each run, Pallas kernels for 0% -> 0%
where the time goes in v1:
time: 73.7 us; the launch traced here: 73.3 us
  waiting for transfers between devices  35.2 us (48%)
  between operations  18.6 us (25%)
  starting transfers between devices  12 us (16%)
  other arithmetic  5.56 us (8%)
  local copies, waits for them, and re-layouts  1.97 us (3%)
    reduce_scatter x1, waiting for transfers between devices, per_device(): mine = lax.psum_scatter(stacks, 'epoch', scatter_dimension=2, tiled=True)  22.9 us
    ppermute x4, waiting for transfers between devices, per_device(): from_left = lax.ppermute(from_left, 'vel', ahead)  8.3 us
    ppermute x3, starting transfers between devices, per_device(): from_right = lax.ppermute(from_right, 'vel', downward)  4.78 us
    ppermute x1, waiting for transfers between devices, extended(): lax.ppermute(lax.slice_in_dim(block, 0, width, axis=dim), axis, backward)  3.93 us
    ppermute x4, starting transfers between devices, per_device(): from_left = lax.ppermute(from_left, 'vel', ahead)  3.55 us
    ppermute x1, starting transfers between devices, extended(): lax.ppermute(lax.slice_in_dim(block, block.shape[dim] - width, None, axis...  2.4 us
    another operation x2, other arithmetic, per_device(): weights = jnp.stack([psf, psf * psf], axis=1)  1.77 us
  transfers between devices with their start and end apart: 10, of which 5 were waited for; matrix products, arithmetic and copies ran while one was open for 1% of the time, Pallas kernels for 0%

profile of v1, /device:TPU:0, one launch (start us, length us, event | category | flops | bytes accessed | tf_op | source)
XLA Modules:
  0.0 73.3 jit_solution(3670587209043674819)
XLA Ops:
  6.5 0.7 multiply_bitcast_fusion
  7.2 1.1 %fusion.26 = (f32[2,2,1]{2,0,1:T(2,128)S(1)}, f32[2,2,1]{2,0,1:T(2,128)S(1)}, f32[2,2,1]{2,0,1:T(2,128)S(1)}, f32[2,2,1]{2,0,1:T(2,128)S(1)}, f32[2,2,1]{2,0,1:T...) fusion(f32[2,1,9]{2,0,1:T(2,128)} %bitcast.48, ...), kind=kLoop, calls=%fused_computation.75 | loop fusion | flops 36 | bytes 288 | tf_op jit(solution)/shard_map/stack | solution.py:49
  8.3 0.1 copy.11
  8.4 0.1 copy.12
  8.5 0.1 copy.13
  8.6 0.1 copy.5
  8.7 0.1 copy.6
  8.8 0.1 copy.7
  8.9 0.1 copy.8
  9.0 0.1 copy.9
  9.1 0.1 copy.10
  9.2 0.8 %divide_bitcast_fusion.1 = (f32[2,1,4,1024]{3,2,1,0:T(4,128)S(1)}, f32[2,1,4,1024]{3,2,1,0:T(4,128)S(1)}) fusion(f32[2,4,1024]{2,1,0:T(4,128)} %param.4, f32[2,4,1024]{2,1,0:T(4,128)} %param.5), kind=kLoop, calls=%fused_computation.45 | loop fusion | flops 16384 | bytes 131072 | tf_op jit(solution)/shard_map/stack | solution.py:48
  10.0 0.0 copy-start
  10.0 0.4 multiply_add_fusion
  10.4 2.4 %collective-permute-start = (f32[2,2,4,1024]{3,2,1,0:T(4,128)S(1)}, f32[2,2,4,1024]{3,2,1,0:T(4,128)S(1)}, u32[]{:S(2)}, u32[]{:S(2)}) collective-permute-start(f32[2,2,4,1024]{3,2,1,0:T(4,128)S(1)} %multiply_add_fusion), channel_id=1, source_target_pairs={{0,1},{1,2},{2,3},{3,4},{4,5},{5,6},{6,7},{8,9},{9,10},{10,11},{11... | collective-permute-start | bytes 196616 | tf_op jit(solution)/shard_map/ppermute | solution.py:14
  12.8 1.3 %collective-permute-start.1 = (f32[2,2,4,1024]{3,2,1,0:T(4,128)S(1)}, f32[2,2,4,1024]{3,2,1,0:T(4,128)S(1)}, u32[]{:S(2)}, u32[]{:S(2)}) collective-permute-start(f32[2,2,4,1024]{3,2,1,0:T(4,128)S(1)} %multiply_add_fusion), channel_id=1, source_target_pairs={{1,0},{2,1},{3,2},{4,3},{5,4},{6,5},{7,6},{9,8},{10,9},{11,10},{12... | collective-permute-start | bytes 196616 | tf_op jit(solution)/shard_map/ppermute | solution.py:17
  14.1 3.9 %collective-permute-done.1 = f32[2,2,4,1024]{3,2,1,0:T(4,128)S(1)} collective-permute-done((f32[2,2,4,1024]{3,2,1,0:T(4,128)S(1)}, f32[2,2,4,1024]{3,2,1,0:T(4,128)S(1)}, u32[]{:S(2)}, u32[]{:S(2)}) %collective-permute-start.1) | collective-permute-done | bytes 65568 | tf_op jit(solution)/shard_map/ppermute | solution.py:17
  18.1 0.3 constant_dynamic-update-slice_fusion.7
  18.4 3.0 %collective-permute-start.2 = (f32[2,2,4,1024]{3,2,1,0:T(4,128)S(1)}, f32[2,2,4,1024]{3,2,1,0:T(4,128)S(1)}, u32[]{:S(2)}, u32[]{:S(2)}) collective-permute-start(f32[2,2,4,1024]{3,2,1,0:T(4,128)S(1)} %get-tuple-element.28), channel_id=1, source_target_pairs={{0,1},{1,2},{2,3},{3,4},{4,5},{5,6},{6,7},{7,0},{8,9},{9,10},{10,1... | collective-permute-start | bytes 196616 | tf_op jit(solution)/shard_map/ppermute | solution.py:63
  21.4 0.0 collective-permute-start.3
  21.4 0.7 constant_dynamic-slice_fusion
  27.1 0.6 collective-permute-start.4
  27.7 2.1 %collective-permute-start.5 = (f32[2,2,4,1024]{3,2,1,0:T(4,128)S(1)}, f32[2,2,4,1024]{3,2,1,0:T(4,128)S(1)}, u32[]{:S(2)}, u32[]{:S(2)}) collective-permute-start(f32[2,2,4,1024]{3,2,1,0:T(4,128)S(1)} %collective-permute-done.3), channel_id=1, source_target_pairs={{0,7},{1,0},{2,1},{3,2},{4,3},{5,4},{6,5},{7,6},{8,15},{9,8},{10,9... | collective-permute-start | bytes 196616 | tf_op jit(solution)/shard_map/ppermute | solution.py:68
  29.9 1.9 %collective-permute-done.4 = f32[2,2,4,1024]{3,2,1,0:T(4,128)S(1)} collective-permute-done((f32[2,2,4,1024]{3,2,1,0:T(4,128)S(1)}, f32[2,2,4,1024]{3,2,1,0:T(4,128)S(1)}, u32[]{:S(2)}, u32[]{:S(2)}) %collective-permute-start.4) | collective-permute-done | bytes 65568 | tf_op jit(solution)/shard_map/ppermute | solution.py:63
  31.8 2.6 %collective-permute-start.7 = (f32[2,2,4,1024]{3,2,1,0:T(4,128)S(1)}, f32[2,2,4,1024]{3,2,1,0:T(4,128)S(1)}, u32[]{:S(2)}, u32[]{:S(2)}) collective-permute-start(f32[2,2,4,1024]{3,2,1,0:T(4,128)S(1)} %collective-permute-done.5), channel_id=1, source_target_pairs={{0,7},{1,0},{2,1},{3,2},{4,3},{5,4},{6,5},{7,6},{8,15},{9,8},{10,9... | collective-permute-start | bytes 196616 | tf_op jit(solution)/shard_map/ppermute | solution.py:68
  34.5 1.9 %collective-permute-done.6 = f32[2,2,4,1024]{3,2,1,0:T(4,128)S(1)} collective-permute-done((f32[2,2,4,1024]{3,2,1,0:T(4,128)S(1)}, f32[2,2,4,1024]{3,2,1,0:T(4,128)S(1)}, u32[]{:S(2)}, u32[]{:S(2)}) %collective-permute-start.6) | collective-permute-done | bytes 65568 | tf_op jit(solution)/shard_map/ppermute | solution.py:63
  36.4 4.5 %collective-permute-done.8 = f32[2,2,4,1024]{3,2,1,0:T(4,128)S(1)} collective-permute-done((f32[2,2,4,1024]{3,2,1,0:T(4,128)S(1)}, f32[2,2,4,1024]{3,2,1,0:T(4,128)S(1)}, u32[]{:S(2)}, u32[]{:S(2)}) %collective-permute-start.8) | collective-permute-done | bytes 65568 | tf_op jit(solution)/shard_map/ppermute | solution.py:63
  41.0 0.2 pad_slice_fusion.1
  41.2 0.9 %dynamic-slice_add_fusion = f32[1,2,32,1024]{3,2,1,0:T(8,128)} fusion(f32[1,2,64,1056]{3,2,1,0:T(8,128)S(1)} %get-tuple-element.30, s32[]{:T(128)} %bitcast.21, s32[]{:T(128)} %bitcast.24, f32[1,2,64,1056]{3,2,1,0:T(8,128)S(1)} %get-tuple-element.29, s32[]{:T(128)} %bitcast.15, s32[]{:T(128)} %bitcast.18), kind=kLoop, calls=%fused_computation.2 | loop fusion | flops 65536 | bytes 786448 | tf_op jit(solution)/shard_map/add | solution.py:84
  42.1 0.0 reduce-scatter.2.cloned.1.call-update
  42.1 22.9 %reduce-scatter.2.cloned.1.call-done = f32[1,2,8,1024]{3,2,1,0:T(8,128)} async-done(((f32[1,2,32,1024]{3,2,1,0:T(8,128)}), f32[1,2,8,1024]{3,2,1,0:T(8,128)}) %reduce-scatter.2.cloned.1.call-update) | async-done | bytes 65552 | tf_op jit(solution)/shard_map/reduce_scatter | solution.py:87
  65.1 1.4 %fusion.24 = f32[1,8,1024]{2,1,0:T(8,128)} fusion(f32[1,2,8,1024]{3,2,1,0:T(8,128)} %reduce-scatter.2.cloned.1.call-done), kind=kLoop, calls=%fused_computation.43 | loop fusion | flops 8192 | bytes 98304 | tf_op jit(solution)/shard_map/div | solution.py:88
  (18 shorter events, 0.2 us)
Async XLA Ops:
  6.5 58.5 %reduce-scatter.2.cloned.1.call-start = ((), (), s32[]{:S(2)}) async-start(), calls=%async_computation.1 | async-start | bytes 327680 | tf_op jit(solution)/shard_map/reduce_scatter | solution.py:87
  10.0 11.4 %copy-start = (s32[2,8,1]{1,2,0:T(1,128)S(1)}, s32[2,8,1]{1,2,0:T(1,128)}, u32[]{:S(2)}) copy-start(s32[2,8,1]{1,2,0:T(1,128)} %param.7) | copy-start | bytes 196
  10.4 3.7 %collective-permute-start = (f32[2,2,4,1024]{3,2,1,0:T(4,128)S(1)}, f32[2,2,4,1024]{3,2,1,0:T(4,128)S(1)}, u32[]{:S(2)}, u32[]{:S(2)}) collective-permute-start(f32[2,2,4,1024]{3,2,1,0:T(4,128)S(1)} %multiply_add_fusion), channel_id=1, source_target_pairs={{0,1},{1,2},{2,3},{3,4},{4,5},{5,6},{6,7},{8,9},{9,10},{10,11},{11... | collective-permute-start | bytes 196616 | tf_op jit(solution)/shard_map/ppermute | solution.py:14
  12.8 5.2 %collective-permute-start.1 = (f32[2,2,4,1024]{3,2,1,0:T(4,128)S(1)}, f32[2,2,4,1024]{3,2,1,0:T(4,128)S(1)}, u32[]{:S(2)}, u32[]{:S(2)}) collective-permute-start(f32[2,2,4,1024]{3,2,1,0:T(4,128)S(1)} %multiply_add_fusion), channel_id=1, source_target_pairs={{1,0},{2,1},{3,2},{4,3},{5,4},{6,5},{7,6},{9,8},{10,9},{11,10},{12... | collective-permute-start | bytes 196616 | tf_op jit(solution)/shard_map/ppermute | solution.py:17
  18.4 8.7 %collective-permute-start.2 = (f32[2,2,4,1024]{3,2,1,0:T(4,128)S(1)}, f32[2,2,4,1024]{3,2,1,0:T(4,128)S(1)}, u32[]{:S(2)}, u32[]{:S(2)}) collective-permute-start(f32[2,2,4,1024]{3,2,1,0:T(4,128)S(1)} %get-tuple-element.28), channel_id=1, source_target_pairs={{0,1},{1,2},{2,3},{3,4},{4,5},{5,6},{6,7},{7,0},{8,9},{9,10},{10,1... | collective-permute-start | bytes 196616 | tf_op jit(solution)/shard_map/ppermute | solution.py:63
  21.4 6.3 %collective-permute-start.3 = (f32[2,2,4,1024]{3,2,1,0:T(4,128)S(1)}, f32[2,2,4,1024]{3,2,1,0:T(4,128)S(1)}, u32[]{:S(2)}, u32[]{:S(2)}) collective-permute-start(f32[2,2,4,1024]{3,2,1,0:T(4,128)S(1)} %get-tuple-element.28), channel_id=1, source_target_pairs={{0,7},{1,0},{2,1},{3,2},{4,3},{5,4},{6,5},{7,6},{8,15},{9,8},{10,9... | collective-permute-start | bytes 196616 | tf_op jit(solution)/shard_map/ppermute | solution.py:68
  27.1 4.6 %collective-permute-start.4 = (f32[2,2,4,1024]{3,2,1,0:T(4,128)S(1)}, f32[2,2,4,1024]{3,2,1,0:T(4,128)S(1)}, u32[]{:S(2)}, u32[]{:S(2)}) collective-permute-start(f32[2,2,4,1024]{3,2,1,0:T(4,128)S(1)} %collective-permute-done.2), channel_id=1, source_target_pairs={{0,1},{1,2},{2,3},{3,4},{4,5},{5,6},{6,7},{7,0},{8,9},{9,10},{10,1... | collective-permute-start | bytes 196616 | tf_op jit(solution)/shard_map/ppermute | solution.py:63
  27.7 4.1 %collective-permute-start.5 = (f32[2,2,4,1024]{3,2,1,0:T(4,128)S(1)}, f32[2,2,4,1024]{3,2,1,0:T(4,128)S(1)}, u32[]{:S(2)}, u32[]{:S(2)}) collective-permute-start(f32[2,2,4,1024]{3,2,1,0:T(4,128)S(1)} %collective-permute-done.3), channel_id=1, source_target_pairs={{0,7},{1,0},{2,1},{3,2},{4,3},{5,4},{6,5},{7,6},{8,15},{9,8},{10,9... | collective-permute-start | bytes 196616 | tf_op jit(solution)/shard_map/ppermute | solution.py:68
  31.8 4.6 %collective-permute-start.6 = (f32[2,2,4,1024]{3,2,1,0:T(4,128)S(1)}, f32[2,2,4,1024]{3,2,1,0:T(4,128)S(1)}, u32[]{:S(2)}, u32[]{:S(2)}) collective-permute-start(f32[2,2,4,1024]{3,2,1,0:T(4,128)S(1)} %collective-permute-done.4), channel_id=1, source_target_pairs={{0,1},{1,2},{2,3},{3,4},{4,5},{5,6},{6,7},{7,0},{8,9},{9,10},{10,1... | collective-permute-start | bytes 196616 | tf_op jit(solution)/shard_map/ppermute | solution.py:63
  31.8 4.6 %collective-permute-start.7 = (f32[2,2,4,1024]{3,2,1,0:T(4,128)S(1)}, f32[2,2,4,1024]{3,2,1,0:T(4,128)S(1)}, u32[]{:S(2)}, u32[]{:S(2)}) collective-permute-start(f32[2,2,4,1024]{3,2,1,0:T(4,128)S(1)} %collective-permute-done.5), channel_id=1, source_target_pairs={{0,7},{1,0},{2,1},{3,2},{4,3},{5,4},{6,5},{7,6},{8,15},{9,8},{10,9... | collective-permute-start | bytes 196616 | tf_op jit(solution)/shard_map/ppermute | solution.py:68
  36.4 4.6 %collective-permute-start.8 = (f32[2,2,4,1024]{3,2,1,0:T(4,128)S(1)}, f32[2,2,4,1024]{3,2,1,0:T(4,128)S(1)}, u32[]{:S(2)}, u32[]{:S(2)}) collective-permute-start(f32[2,2,4,1024]{3,2,1,0:T(4,128)S(1)} %collective-permute-done.6), channel_id=1, source_target_pairs={{0,1},{1,2},{2,3},{3,4},{4,5},{5,6},{6,7},{7,0},{8,9},{9,10},{10,1... | collective-permute-start | bytes 196616 | tf_op jit(solution)/shard_map/ppermute | solution.py:63
Sparse Core Ops, SparseCore 0:
  42.3 22.7 reduce-scatter.1
